TPU v7x, 128 devices: a whole 4x4x4 slice. The times are simulated.
128 devices in a mesh: cell: 16 (over x, z_hi, core), tm: 8 (over y, z_lo).
Axes of the slice: x: 4, y: 4, z: 4 (z_hi: 2, z_lo: 2; z = z_hi * 2 + z_lo), core: 2. Of those that a mesh axis runs over, the one named last changes fastest.
Arguments:
- window: float32 [16384, 16384], P('cell', 'tm'), may hold values from -0.09375 to 0.09375
- range_test: float32 [16384, 256], P('tm'), may hold values from -0.046875 to 0.046875
- co_test: float32 [256, 16384], P(None, 'cell'), may hold values from -0.046875 to 0.046875
- core_left: float32 [512, 16384], P(None, 'cell'), may hold values from -0.046875 to 0.046875
- core_right: float32 [512, 16384], P(None, 'tm'), may hold values from -0.046875 to 0.046875
Outputs:
- range_basis: float32 [16384, 256], P('cell')
- co_basis: float32 [256, 16384], P(None, 'tm')
- core: float32 [256, 256], replicated
All inputs are finite; a program needn't handle non-finite values.
Results may differ from a plain program's by a relative error of at most 0.00023.
Values sent between devices are 32-bit elements; how exact they have to be, the bound alone decides.
A program may use at most 128 MiB of HBM per device.

v0:
```python
import math
import jax
import jax.numpy as jnp
from jax import lax
from jax.sharding import PartitionSpec as P


def inner_rows(left, right):
    return lax.dot_general(left, right, (((0,), (0,)), ((), ())), precision=lax.Precision.HIGHEST)


def inner_cols(left, right):
    return lax.dot_general(left, right, (((1,), (1,)), ((), ())), precision=lax.Precision.HIGHEST)


def product(left, right):
    return jnp.dot(left, right, precision=lax.Precision.HIGHEST, preferred_element_type=jnp.float32)


def per_device(window, range_test, co_test, core_left, core_right):
    rows_total = window.shape[0] * lax.axis_size("cell")
    cols_total = window.shape[1] * lax.axis_size("tm")
    range_term = product(window, range_test)
    co_term = product(co_test, window)
    left_window = product(core_left, window)
    core_term = inner_cols(left_window, core_right)
    sketch_z = lax.psum(core_term, ("cell", "tm"))
    range_full = lax.psum(range_term, "tm")
    co_full = lax.psum(co_term, "cell")
    gram_y = lax.psum(inner_rows(range_full, range_full) / rows_total, "cell")
    gram_w = lax.psum(inner_cols(co_full, co_full) / cols_total, "tm")
    lower_y = jnp.linalg.cholesky(gram_y)
    lower_w = jnp.linalg.cholesky(gram_w)
    range_basis = jax.scipy.linalg.solve_triangular(lower_y, range_full.T, lower=True).T
    co_basis = jax.scipy.linalg.solve_triangular(lower_w, co_full, lower=True)
    left_image = lax.psum(product(core_left, range_basis), "cell")
    right_image = lax.psum(inner_cols(core_right, co_basis), "tm")
    gram_left = inner_rows(left_image, left_image)
    gram_right = inner_rows(right_image, right_image)
    projected = inner_rows(left_image, sketch_z)
    left_solved = jax.scipy.linalg.cho_solve((jnp.linalg.cholesky(gram_left), True), projected)
    middle = product(left_solved, right_image)
    core = jax.scipy.linalg.cho_solve((jnp.linalg.cholesky(gram_right), True), middle.T).T
    core = core * math.sqrt(rows_total * cols_total)
    return (range_basis, co_basis, core)


def solution(mesh):
    return jax.shard_map(
        per_device,
        mesh=mesh,
        in_specs=(P("cell", "tm"), P("tm", None), P(None, "cell"), P(None, "cell"), P(None, "tm")),
        out_specs=(P("cell", None), P(None, "tm"), P()),
        check_vma=False,
    )
```

profile of v0, /device:TPU:0, one launch (start us, length us, event | category | flops | bytes accessed | tf_op | source)
XLA Modules:
  0.0 920.8 jit_solution(13198876106782574047)
XLA Ops:
  7.2 10.7 %fusion.50 = f32[1024,256]{1,0:T(8,128)} fusion(f32[1024,2048]{1,0:T(8,128)} %param.6, f32[2048,256]{1,0:T(8,128)} %param.7), kind=kOutput, calls=%fused_computation.123 | convolution fusion | flops 6442450944 | bytes 11534336 | tf_op jit(solution)/shard_map/dot_general | solution.py:17
  18.0 80.7 %all-reduce.9.cloned.1.call-done = f32[1024,256]{1,0:T(8,128)} async-done(((f32[1024,256]{1,0:T(8,128)}), f32[1024,256]{1,0:T(8,128)}) %all-reduce.9.cloned.1.call-update) | async-done | bytes 1048592 | tf_op jit(solution)/shard_map/psum | solution.py:28
  98.6 4.1 convolution_multiply_fusion.1
  102.8 10.7 %fusion.51 = f32[256,2048]{1,0:T(8,128)} fusion(f32[256,1024]{1,0:T(8,128)S(1)} %copy-done.12, f32[1024,2048]{1,0:T(8,128)} %param.6), kind=kOutput, calls=%fused_computation.124 | convolution fusion | flops 6442450944 | bytes 11534336 | tf_op jit(solution)/shard_map/dot_general | solution.py:17
  113.5 127.4 %all-reduce.11.cloned.1.call-done = f32[256,256]{0,1:T(8,128)} async-done(((f32[256,256]{0,1:T(8,128)}), f32[256,256]{0,1:T(8,128)}) %all-reduce.11.cloned.1.call-update) | async-done | bytes 262160 | tf_op jit(solution)/shard_map/psum | solution.py:30
  243.7 11.7 %cholesky.214 = f32[128,128]{1,0:T(8,128)S(1)} custom-call(f32[128,128]{1,0:T(8,128)S(1)} %cholesky.346), custom_call_target="Cholesky" | custom-call | tf_op jit(solution)/shard_map/jit(cholesky)/cholesky | solution.py:32
  255.5 9.8 %custom-call.37 = f32[1,128,128]{1,2,0:T(8,128)S(1)} custom-call(f32[1,128,128]{2,1,0:T(8,128)S(1)} %get-tuple-element.96), custom_call_target="InvertDiagBlocksLowerTriangular" | custom-call | tf_op jit(solution)/shard_map/jit(cholesky)/cholesky | solution.py:32
  267.4 11.7 %cholesky.231 = f32[128,128]{1,0:T(8,128)S(1)} custom-call(f32[128,128]{1,0:T(8,128)S(1)} %convolution_subtract_fusion.9), custom_call_target="Cholesky" | custom-call | tf_op jit(solution)/shard_map/jit(cholesky)/cholesky | solution.py:32
  282.3 4.1 while.4
  287.0 20.7 %custom-call.30 = f32[2,128,128]{1,2,0:T(8,128)S(1)} custom-call(f32[2,128,128]{2,1,0:T(8,128)} %copy-done.17), custom_call_target="InvertDiagBlocksLowerTriangular" | custom-call | tf_op jit(solution)/shard_map/jit(_solve_triangular)/triangular_solve | solution.py:34
  312.9 16.9 %fusion.54 = f32[512,2048]{1,0:T(8,128)S(1)} fusion(f32[512,1024]{1,0:T(8,128)S(1)} %copy-done, f32[1024,2048]{1,0:T(8,128)} %param.6), kind=kOutput, calls=%fused_computation.127 | convolution fusion | flops 12884901888 | bytes 14680064 | tf_op jit(solution)/shard_map/dot_general | solution.py:17
  329.8 7.9 fusion.55
  344.1 116.8 %all-reduce.19.cloned.1.call-done = (f32[256,2048]{1,0:T(8,128)}, f32[512,256]{0,1:T(8,128)}) async-done(((f32[256,2048]{1,0:T(8,128)}, f32[512,256]{0,1:T(8,128)}), (f32[256,2048]{1,0:T(8,128)}, f32[512,256]{0,1:T(8,128)})) %all-reduce.19.cloned.1.call-update) | async-done | bytes 2621456 | tf_op jit(solution)/shard_map/psum | solution.py:29
  462.9 11.7 %cholesky.316 = f32[128,128]{1,0:T(8,128)S(1)} custom-call(f32[128,128]{1,0:T(8,128)S(1)} %cholesky.355), custom_call_target="Cholesky" | custom-call | tf_op jit(solution)/shard_map/jit(cholesky)/cholesky | solution.py:41
  474.7 9.8 %custom-call.40 = f32[1,128,128]{1,2,0:T(8,128)S(1)} custom-call(f32[1,128,128]{2,1,0:T(8,128)S(1)} %get-tuple-element.88), custom_call_target="InvertDiagBlocksLowerTriangular" | custom-call | tf_op jit(solution)/shard_map/jit(cholesky)/cholesky | solution.py:41
  485.0 11.7 %cholesky.333 = f32[128,128]{1,0:T(8,128)S(1)} custom-call(f32[128,128]{1,0:T(8,128)S(1)} %convolution_subtract_fusion.6), custom_call_target="Cholesky" | custom-call | tf_op jit(solution)/shard_map/jit(cholesky)/cholesky | solution.py:41
  499.5 4.1 while.7
  503.6 19.7 %custom-call.33 = f32[2,128,128]{1,2,0:T(8,128)S(1)} custom-call(f32[2,128,128]{2,1,0:T(8,128)S(1)} %get-tuple-element.35), custom_call_target="InvertDiagBlocksLowerTriangular" | custom-call | tf_op jit(solution)/shard_map/jit(_cho_solve)/triangular_solve | solution.py:41
  523.3 4.8 convolution_multiply_fusion
  528.6 85.9 %all-reduce.17.cloned.1.call-done = f32[512,512]{1,0:T(8,128)} async-done(((f32[512,512]{1,0:T(8,128)}), f32[512,512]{1,0:T(8,128)}) %all-reduce.17.cloned.1.call-update) | async-done | bytes 1048592 | tf_op jit(solution)/shard_map/psum | solution.py:27
  618.1 73.0 %all-reduce.13.cloned.1.call-done = f32[256,256]{0,1:T(8,128)} async-done(((f32[256,256]{0,1:T(8,128)}), f32[256,256]{0,1:T(8,128)}) %all-reduce.13.cloned.1.call-update) | async-done | bytes 262160 | tf_op jit(solution)/shard_map/psum | solution.py:31
  693.2 11.7 %cholesky.248 = f32[128,128]{1,0:T(8,128)S(1)} custom-call(f32[128,128]{1,0:T(8,128)S(1)} %cholesky.349), custom_call_target="Cholesky" | custom-call | tf_op jit(solution)/shard_map/jit(cholesky)/cholesky | solution.py:33
  705.0 9.8 %custom-call.38 = f32[1,128,128]{1,2,0:T(8,128)S(1)} custom-call(f32[1,128,128]{2,1,0:T(8,128)S(1)} %get-tuple-element.92), custom_call_target="InvertDiagBlocksLowerTriangular" | custom-call | tf_op jit(solution)/shard_map/jit(cholesky)/cholesky | solution.py:33
  716.9 11.9 %cholesky.265 = f32[128,128]{1,0:T(8,128)S(1)} custom-call(f32[128,128]{1,0:T(8,128)S(1)} %convolution_subtract_fusion.8), custom_call_target="Cholesky" | custom-call | tf_op jit(solution)/shard_map/jit(cholesky)/cholesky | solution.py:33
  735.5 19.7 %custom-call.31 = f32[2,128,128]{1,2,0:T(8,128)S(1)} custom-call(f32[2,128,128]{2,1,0:T(8,128)S(1)} %get-tuple-element.19), custom_call_target="InvertDiagBlocksLowerTriangular" | custom-call | tf_op jit(solution)/shard_map/jit(_solve_triangular)/triangular_solve | solution.py:35
  762.6 4.5 convolution_bitcast_fusion.1
  768.3 73.2 %all-reduce.15.cloned.1.call-done = f32[512,256]{0,1:T(8,128)} async-done(((f32[512,256]{0,1:T(8,128)}), f32[512,256]{0,1:T(8,128)}) %all-reduce.15.cloned.1.call-update) | async-done | bytes 524304 | tf_op jit(solution)/shard_map/psum | solution.py:37
  845.9 11.9 %cholesky.282 = f32[128,128]{1,0:T(8,128)S(1)} custom-call(f32[128,128]{1,0:T(8,128)S(1)} %cholesky.352), custom_call_target="Cholesky" | custom-call | tf_op jit(solution)/shard_map/jit(cholesky)/cholesky | solution.py:43
  857.8 9.8 %custom-call.39 = f32[1,128,128]{1,2,0:T(8,128)S(1)} custom-call(f32[1,128,128]{2,1,0:T(8,128)S(1)} %get-tuple-element.84), custom_call_target="InvertDiagBlocksLowerTriangular" | custom-call | tf_op jit(solution)/shard_map/jit(cholesky)/cholesky | solution.py:43
  869.8 11.7 %cholesky.299 = f32[128,128]{1,0:T(8,128)S(1)} custom-call(f32[128,128]{1,0:T(8,128)S(1)} %convolution_subtract_fusion.7), custom_call_target="Cholesky" | custom-call | tf_op jit(solution)/shard_map/jit(cholesky)/cholesky | solution.py:43
  885.2 4.1 while.6
  890.0 20.5 %custom-call.32 = f32[2,128,128]{1,2,0:T(8,128)S(1)} custom-call(f32[2,128,128]{2,1,0:T(8,128)} %copy-done.16), custom_call_target="InvertDiagBlocksLowerTriangular" | custom-call | tf_op jit(solution)/shard_map/jit(_cho_solve)/triangular_solve | solution.py:43
  (150 shorter events, 74.1 us)
Async XLA Ops:
  7.2 302.9 %copy-start = (f32[512,1024]{1,0:T(8,128)S(1)}, f32[512,1024]{1,0:T(8,128)}, u32[]{:S(2)}) copy-start(f32[512,1024]{1,0:T(8,128)} %param.9) | copy-start | bytes 6291460
  7.2 91.5 %all-reduce.9.cloned.1.call-start = ((), (), s32[]{:S(2)}) async-start(), calls=%async_computation | async-start | bytes 2097152 | tf_op jit(solution)/shard_map/psum | solution.py:28
  17.9 84.9 %copy-start.12 = (f32[256,1024]{1,0:T(8,128)S(1)}, f32[256,1024]{1,0:T(8,128)}, u32[]{:S(2)}) copy-start(f32[256,1024]{1,0:T(8,128)} %param.8) | copy-start | bytes 3145732
  17.9 223.0 %all-reduce.11.cloned.1.call-start = ((), (), s32[]{:S(2)}) async-start(), calls=%async_computation.1 | async-start | bytes 524288 | tf_op jit(solution)/shard_map/psum | solution.py:30
  102.7 358.2 %all-reduce.19.cloned.1.call-start = ((), (), s32[]{:S(2)}) async-start(), calls=%async_computation.5 | async-start | bytes 5242880 | tf_op jit(solution)/shard_map/psum | solution.py:29
  113.5 194.2 %copy-start.4 = (f32[1024,256]{1,0:T(8,128)S(1)}, f32[1024,256]{1,0:T(8,128)}, u32[]{:S(2)}) copy-start(f32[1024,256]{1,0:T(8,128)} %all-reduce.9.cloned.1.call-done) | copy-start | bytes 3145732
  243.0 0.7 copy-start.13
  279.2 2.0 copy-start.10
  286.4 0.7 copy-start.17
  308.4 1.7 copy-start.5
  312.8 301.7 %all-reduce.17.cloned.1.call-start = ((), (), s32[]{:S(2)}) async-start(), calls=%async_computation.4 | async-start | bytes 2097152 | tf_op jit(solution)/shard_map/psum | solution.py:27
  312.9 16.9 %copy-start.2 = (f32[512,2048]{1,0:T(8,128)S(1)}, f32[512,2048]{1,0:T(8,128)}, u32[]{:S(2)}) copy-start(f32[512,2048]{1,0:T(8,128)} %param.10) | copy-start | bytes 12582916
  329.8 10.7 %copy-start.6 = (f32[128,1024]{1,0:T(8,128)S(1)}, f32[128,1024]{1,0:T(8,128)}, u32[]{:S(2)}) copy-start(f32[128,1024]{1,0:T(8,128)} %copy-done.5) | copy-start | bytes 1572868
  337.7 353.3 %all-reduce.13.cloned.1.call-start = ((), (), s32[]{:S(2)}) async-start(), calls=%async_computation.2 | async-start | bytes 524288 | tf_op jit(solution)/shard_map/psum | solution.py:31
  523.3 91.3 %copy-start.9 = (f32[512,256]{0,1:T(8,128)S(1)}, f32[512,256]{0,1:T(8,128)}, u32[]{:S(2)}) copy-start(f32[512,256]{0,1:T(8,128)} %get-tuple-element.72) | copy-start | bytes 1572868
  528.2 313.4 %all-reduce.15.cloned.1.call-start = ((), (), s32[]{:S(2)}) async-start(), calls=%async_computation.3 | async-start | bytes 1048576 | tf_op jit(solution)/shard_map/psum | solution.py:37
  693.2 11.7 %copy-start.14 = (f32[256,256]{1,0:T(8,128)}, f32[256,256]{1,0:T(8,128)S(1)}, u32[]{:S(2)}) copy-start(f32[256,256]{1,0:T(8,128)S(1)} %fusion.14) | copy-start | bytes 786436
  755.2 2.4 copy-start.1
  759.7 2.9 copy-start.3
  759.9 1.3 copy-start.7
  843.3 67.1 %copy-start.8 = (f32[512,256]{0,1:T(8,128)S(1)}, f32[512,256]{0,1:T(8,128)}, u32[]{:S(2)}) copy-start(f32[512,256]{0,1:T(8,128)} %all-reduce.15.cloned.1.call-done) | copy-start | bytes 1572868
  845.2 0.7 copy-start.15
  882.3 1.9 copy-start.11
  889.3 0.7 copy-start.16
Sparse Core Ops, SparseCore 0:
  18.1 80.5 all-reduce.8
  102.8 138.0 all-reduce.10
  313.0 147.9 all-reduce.18
  465.6 148.9 all-reduce.16
  617.4 73.6 all-reduce.12
  767.3 74.1 all-reduce.14
where the time goes:
time: 929 us; the launch traced here: 921 us
  waiting for transfers between devices  557 us (60%)
  other arithmetic  225 us (24%)
  matrix products  86.6 us (9%)
  local copies, waits for them, and re-layouts  28.3 us (3%)
  between operations  20.2 us (2%)
    psum x1, waiting for transfers between devices, per_device(): gram_y = lax.psum(inner_rows(range_full, range_full) / rows_total, 'cell')  127 us
    psum x1, waiting for transfers between devices, per_device(): co_full = lax.psum(co_term, 'cell')  117 us
    psum x1, waiting for transfers between devices, per_device(): sketch_z = lax.psum(core_term, ('cell', 'tm'))  85.9 us
    psum x1, waiting for transfers between devices, per_device(): range_full = lax.psum(range_term, 'tm')  80.7 us
    psum x1, waiting for transfers between devices, per_device(): right_image = lax.psum(inner_cols(core_right, co_basis), 'tm')  73.2 us
    psum x1, waiting for transfers between devices, per_device(): gram_w = lax.psum(inner_cols(co_full, co_full) / cols_total, 'tm')  73 us
    dot_general x5, matrix products, product(): jnp.dot(left, right, precision=lax.Precision.HIGHEST, preferred_element_t...  41.6 us
    another operation x7, other arithmetic, per_device(): jnp.linalg.cholesky(gram_right)  34.8 us
  transfers between devices with their start and end apart: 6, of which 6 were waited for; matrix products, arithmetic and copies ran while one was open for 12% of the time, Pallas kernels for 0%

commit v1 on v0

--- a/solution.py
+++ b/solution.py
@@ -24,7 +24,9 @@
     co_term = product(co_test, window)
     left_window = product(core_left, window)
     core_term = inner_cols(left_window, core_right)
-    sketch_z = lax.psum(core_term, ("cell", "tm"))
+    sketch_z = core_term
+    for over in ("cell", "tm"):
+        sketch_z = lax.psum(sketch_z, over)
     range_full = lax.psum(range_term, "tm")
     co_full = lax.psum(co_term, "cell")
     gram_y = lax.psum(inner_rows(range_full, range_full) / rows_total, "cell")

time: 929 us -> 791 us (0.85)
  waiting for transfers between devices: 557 us -> 428 us
    psum x1 -> x0, waiting for transfers between devices: 85.9 us -> none  [per_device(): sketch_z = lax.psum(core_term, ('cell', 'tm'))]
    psum x1, waiting for transfers between devices: 117 us -> 148 us  [per_device(): co_full = lax.psum(co_term, 'cell')]
    psum x1, waiting for transfers between devices: 80.7 us -> 54.6 us  [per_device(): range_full = lax.psum(range_term, 'tm')]
    psum x1, waiting for transfers between devices: 73.2 us -> 48.1 us  [per_device(): right_image = lax.psum(inner_cols(core_right, co_basis), 'tm')]
    psum x1, waiting for transfers between devices: 73 us -> 50.2 us  [per_device(): gram_w = lax.psum(inner_cols(co_full, co_full) / cols_total, 'tm')]
  transfers between devices with their start and end apart: 6 -> 5, of which waited for: 6 -> 5; matrix products, arithmetic and copies ran while one was open for 12% -> 13% of each run, Pallas kernels for 0% -> 0%
where the time goes in v1:
time: 791 us; the launch traced here: 787 us
  waiting for transfers between devices  428 us (54%)
  other arithmetic  223 us (28%)
  matrix products  87.9 us (11%)
  local copies, waits for them, and re-layouts  27.1 us (3%)
  between operations  19.6 us (2%)
    psum x1, waiting for transfers between devices, per_device(): co_full = lax.psum(co_term, 'cell')  148 us
    psum x1, waiting for transfers between devices, per_device(): gram_y = lax.psum(inner_rows(range_full, range_full) / rows_total, 'cell')  128 us
    psum x1, waiting for transfers between devices, per_device(): range_full = lax.psum(range_term, 'tm')  54.6 us
    psum x1, waiting for transfers between devices, per_device(): gram_w = lax.psum(inner_cols(co_full, co_full) / cols_total, 'tm')  50.2 us
    psum x1, waiting for transfers between devices, per_device(): right_image = lax.psum(inner_cols(core_right, co_basis), 'tm')  48.1 us
    dot_general x5, matrix products, product(): jnp.dot(left, right, precision=lax.Precision.HIGHEST, preferred_element_t...  40.1 us
    another operation x7, other arithmetic, per_device(): lower_w = jnp.linalg.cholesky(gram_w)  34.8 us
    another operation x7, other arithmetic, per_device(): jnp.linalg.cholesky(gram_right)  34.6 us
  transfers between devices with their start and end apart: 5, of which 5 were waited for; matrix products, arithmetic and copies ran while one was open for 13% of the time, Pallas kernels for 0%

profile of v1, /device:TPU:0, one launch (start us, length us, event | category | flops | bytes accessed | tf_op | source)
XLA Modules:
  0.0 786.8 jit_solution(13894511482792279274)
XLA Ops:
  7.2 10.7 %fusion.50 = f32[1024,256]{1,0:T(8,128)} fusion(f32[1024,2048]{1,0:T(8,128)} %param.6, f32[2048,256]{1,0:T(8,128)} %param.7), kind=kOutput, calls=%fused_computation.123 | convolution fusion | flops 6442450944 | bytes 11534336 | tf_op jit(solution)/shard_map/dot_general | solution.py:17
  18.2 10.7 %fusion.51 = f32[256,2048]{1,0:T(8,128)} fusion(f32[256,1024]{1,0:T(8,128)S(1)} %copy-done.11, f32[1024,2048]{1,0:T(8,128)} %param.6), kind=kOutput, calls=%fused_computation.124 | convolution fusion | flops 6442450944 | bytes 11534336 | tf_op jit(solution)/shard_map/dot_general | solution.py:17
  29.0 15.2 %fusion.54 = f32[512,2048]{1,0:T(8,128)} fusion(f32[512,1024]{1,0:T(8,128)S(1)} %copy-done, f32[1024,2048]{1,0:T(8,128)S(1)} %copy-done.1), kind=kOutput, calls=%fused_computation.127 | convolution fusion | flops 12884901888 | bytes 14680064 | tf_op jit(solution)/shard_map/dot_general | solution.py:17
  44.2 54.6 %all-reduce.9.cloned.1.call-done = f32[1024,256]{1,0:T(8,128)} async-done(((f32[1024,256]{1,0:T(8,128)}), f32[1024,256]{1,0:T(8,128)}) %all-reduce.9.cloned.1.call-update) | async-done | bytes 1048592 | tf_op jit(solution)/shard_map/psum | solution.py:30
  98.8 4.1 convolution_multiply_fusion.1
  103.1 10.3 %fusion.55 = f32[512,512]{1,0:T(8,128)} fusion(f32[512,2048]{1,0:T(8,128)} %fusion.54, f32[512,2048]{1,0:T(8,128)} %param.10), kind=kOutput, calls=%fused_computation.128 | convolution fusion | flops 6442450944 | bytes 9437184 | tf_op jit(solution)/shard_map/dot_general | solution.py:13
  113.4 127.6 %all-reduce.11.cloned.1.call-done = f32[256,256]{0,1:T(8,128)} async-done(((f32[256,256]{0,1:T(8,128)}), f32[256,256]{0,1:T(8,128)}) %all-reduce.11.cloned.1.call-update) | async-done | bytes 262160 | tf_op jit(solution)/shard_map/psum | solution.py:32
  243.8 11.7 %cholesky.214 = f32[128,128]{1,0:T(8,128)S(1)} custom-call(f32[128,128]{1,0:T(8,128)S(1)} %cholesky.346), custom_call_target="Cholesky" | custom-call | tf_op jit(solution)/shard_map/jit(cholesky)/cholesky | solution.py:34
  255.6 9.8 %custom-call.37 = f32[1,128,128]{1,2,0:T(8,128)S(1)} custom-call(f32[1,128,128]{2,1,0:T(8,128)S(1)} %get-tuple-element.99), custom_call_target="InvertDiagBlocksLowerTriangular" | custom-call | tf_op jit(solution)/shard_map/jit(cholesky)/cholesky | solution.py:34
  267.6 11.7 %cholesky.231 = f32[128,128]{1,0:T(8,128)S(1)} custom-call(f32[128,128]{1,0:T(8,128)S(1)} %convolution_subtract_fusion.9), custom_call_target="Cholesky" | custom-call | tf_op jit(solution)/shard_map/jit(cholesky)/cholesky | solution.py:34
  282.3 3.9 while.4
  286.8 20.9 %custom-call.30 = f32[2,128,128]{1,2,0:T(8,128)S(1)} custom-call(f32[2,128,128]{2,1,0:T(8,128)} %copy-done.16), custom_call_target="InvertDiagBlocksLowerTriangular" | custom-call | tf_op jit(solution)/shard_map/jit(_solve_triangular)/triangular_solve | solution.py:36
  317.4 147.7 %all-reduce.15.cloned.1.call-done = (f32[256,2048]{1,0:T(8,128)}, f32[512,256]{0,1:T(8,128)}, f32[512,512]{1,0:T(8,128)}) async-done(((f32[256,2048]{1,0:T(8,128)}, f32[512,256]{0,1:T(8,128)}, f32[512,512]{1,0:T(8,128)}), (f32[256,2048]{1,0:T(8,128)}, f32[512,256]{0,1:T(8,128)}, f32[512,512]{1,0:T(8,128)})) %all-reduce.15.cloned.1.call-update) | async-done | bytes 3670032 | tf_op jit(solution)/shard_map/psum | solution.py:31
  465.2 4.8 convolution_multiply_fusion
  471.8 11.7 %cholesky.316 = f32[128,128]{1,0:T(8,128)S(1)} custom-call(f32[128,128]{1,0:T(8,128)S(1)} %cholesky.355), custom_call_target="Cholesky" | custom-call | tf_op jit(solution)/shard_map/jit(cholesky)/cholesky | solution.py:43
  483.6 9.8 %custom-call.40 = f32[1,128,128]{1,2,0:T(8,128)S(1)} custom-call(f32[1,128,128]{2,1,0:T(8,128)S(1)} %get-tuple-element.91), custom_call_target="InvertDiagBlocksLowerTriangular" | custom-call | tf_op jit(solution)/shard_map/jit(cholesky)/cholesky | solution.py:43
  494.4 50.2 %all-reduce.13.cloned.1.call-done = f32[256,256]{0,1:T(8,128)} async-done(((f32[256,256]{0,1:T(8,128)}), f32[256,256]{0,1:T(8,128)}) %all-reduce.13.cloned.1.call-update) | async-done | bytes 262160 | tf_op jit(solution)/shard_map/psum | solution.py:33
  546.7 11.7 %cholesky.248 = f32[128,128]{1,0:T(8,128)S(1)} custom-call(f32[128,128]{1,0:T(8,128)S(1)} %cholesky.349), custom_call_target="Cholesky" | custom-call | tf_op jit(solution)/shard_map/jit(cholesky)/cholesky | solution.py:35
  558.5 10.0 %custom-call.38 = f32[1,128,128]{1,2,0:T(8,128)S(1)} custom-call(f32[1,128,128]{2,1,0:T(8,128)S(1)} %get-tuple-element.95), custom_call_target="InvertDiagBlocksLowerTriangular" | custom-call | tf_op jit(solution)/shard_map/jit(cholesky)/cholesky | solution.py:35
  570.6 11.7 %cholesky.265 = f32[128,128]{1,0:T(8,128)S(1)} custom-call(f32[128,128]{1,0:T(8,128)S(1)} %convolution_subtract_fusion.8), custom_call_target="Cholesky" | custom-call | tf_op jit(solution)/shard_map/jit(cholesky)/cholesky | solution.py:35
  585.0 4.0 while.5
  589.0 20.1 %custom-call.31 = f32[2,128,128]{1,2,0:T(8,128)S(1)} custom-call(f32[2,128,128]{2,1,0:T(8,128)S(1)} %get-tuple-element.19), custom_call_target="InvertDiagBlocksLowerTriangular" | custom-call | tf_op jit(solution)/shard_map/jit(_solve_triangular)/triangular_solve | solution.py:37
  615.8 4.5 convolution_bitcast_fusion.1
  621.4 11.7 %cholesky.333 = f32[128,128]{1,0:T(8,128)S(1)} custom-call(f32[128,128]{1,0:T(8,128)S(1)} %convolution_subtract_fusion.6), custom_call_target="Cholesky" | custom-call | tf_op jit(solution)/shard_map/jit(cholesky)/cholesky | solution.py:43
  635.7 3.8 while.7
  639.5 19.8 %custom-call.33 = f32[2,128,128]{1,2,0:T(8,128)S(1)} custom-call(f32[2,128,128]{2,1,0:T(8,128)S(1)} %get-tuple-element.35), custom_call_target="InvertDiagBlocksLowerTriangular" | custom-call | tf_op jit(solution)/shard_map/jit(_cho_solve)/triangular_solve | solution.py:43
  659.3 48.1 %all-reduce.17.cloned.1.call-done = (f32[512,256]{0,1:T(8,128)}, f32[512,512]{1,0:T(8,128)}) async-done(((f32[512,256]{0,1:T(8,128)}, f32[512,512]{1,0:T(8,128)}), (f32[512,256]{0,1:T(8,128)}, f32[512,512]{1,0:T(8,128)})) %all-reduce.17.cloned.1.call-update) | async-done | bytes 1572880 | tf_op jit(solution)/shard_map/psum | solution.py:39
  710.2 11.7 %cholesky.282 = f32[128,128]{1,0:T(8,128)S(1)} custom-call(f32[128,128]{1,0:T(8,128)S(1)} %cholesky.352), custom_call_target="Cholesky" | custom-call | tf_op jit(solution)/shard_map/jit(cholesky)/cholesky | solution.py:45
  721.9 9.8 %custom-call.39 = f32[1,128,128]{1,2,0:T(8,128)S(1)} custom-call(f32[1,128,128]{2,1,0:T(8,128)S(1)} %get-tuple-element.87), custom_call_target="InvertDiagBlocksLowerTriangular" | custom-call | tf_op jit(solution)/shard_map/jit(cholesky)/cholesky | solution.py:45
  733.9 11.7 %cholesky.299 = f32[128,128]{1,0:T(8,128)S(1)} custom-call(f32[128,128]{1,0:T(8,128)S(1)} %convolution_subtract_fusion.7), custom_call_target="Cholesky" | custom-call | tf_op jit(solution)/shard_map/jit(cholesky)/cholesky | solution.py:45
  748.3 3.9 while.6
  752.2 19.9 %custom-call.32 = f32[2,128,128]{1,2,0:T(8,128)S(1)} custom-call(f32[2,128,128]{2,1,0:T(8,128)S(1)} %get-tuple-element.27), custom_call_target="InvertDiagBlocksLowerTriangular" | custom-call | tf_op jit(solution)/shard_map/jit(_cho_solve)/triangular_solve | solution.py:45
  (145 shorter events, 64.6 us)
Async XLA Ops:
  7.2 21.8 %copy-start = (f32[512,1024]{1,0:T(8,128)S(1)}, f32[512,1024]{1,0:T(8,128)}, u32[]{:S(2)}) copy-start(f32[512,1024]{1,0:T(8,128)} %param.9) | copy-start | bytes 6291460
  7.2 11.0 %copy-start.11 = (f32[256,1024]{1,0:T(8,128)S(1)}, f32[256,1024]{1,0:T(8,128)}, u32[]{:S(2)}) copy-start(f32[256,1024]{1,0:T(8,128)} %param.8) | copy-start | bytes 3145732
  7.2 91.6 %all-reduce.9.cloned.1.call-start = ((), (), s32[]{:S(2)}) async-start(), calls=%async_computation | async-start | bytes 2097152 | tf_op jit(solution)/shard_map/psum | solution.py:30
  18.0 223.1 %all-reduce.11.cloned.1.call-start = ((), (), s32[]{:S(2)}) async-start(), calls=%async_computation.1 | async-start | bytes 524288 | tf_op jit(solution)/shard_map/psum | solution.py:32
  18.2 10.7 %copy-start.1 = (f32[1024,2048]{1,0:T(8,128)S(1)}, f32[1024,2048]{1,0:T(8,128)}, u32[]{:S(2)}) copy-start(f32[1024,2048]{1,0:T(8,128)} %param.6) | copy-start | bytes 25165828
  102.9 362.3 %all-reduce.15.cloned.1.call-start = ((), (), s32[]{:S(2)}) async-start(), calls=%async_computation.3 | async-start | bytes 7340032 | tf_op jit(solution)/shard_map/psum | solution.py:31
  113.4 194.3 %copy-start.4 = (f32[1024,256]{1,0:T(8,128)S(1)}, f32[1024,256]{1,0:T(8,128)}, u32[]{:S(2)}) copy-start(f32[1024,256]{1,0:T(8,128)} %all-reduce.9.cloned.1.call-done) | copy-start | bytes 3145732
  243.1 0.7 copy-start.13
  279.4 1.9 copy-start.10
  286.2 0.7 copy-start.16
  308.4 1.7 copy-start.5
  312.8 1.0 copy-start.6
  312.8 231.7 %all-reduce.13.cloned.1.call-start = ((), (), s32[]{:S(2)}) async-start(), calls=%async_computation.2 | async-start | bytes 524288 | tf_op jit(solution)/shard_map/psum | solution.py:33
  465.2 5.1 copy-start.9
  470.0 237.4 %all-reduce.17.cloned.1.call-start = ((), (), s32[]{:S(2)}) async-start(), calls=%async_computation.4 | async-start | bytes 3145728 | tf_op jit(solution)/shard_map/psum | solution.py:39
  471.1 0.7 copy-start.12
  546.7 11.7 %copy-start.14 = (f32[256,256]{1,0:T(8,128)}, f32[256,256]{1,0:T(8,128)S(1)}, u32[]{:S(2)}) copy-start(f32[256,256]{1,0:T(8,128)S(1)} %fusion.14) | copy-start | bytes 786436
  609.1 2.4 copy-start.2
  613.6 2.2 copy-start.3
  615.8 4.5 copy-start.7
  709.4 0.7 copy-start.15
  774.4 2.4 copy-start.8
Sparse Core Ops, SparseCore 0:
  18.1 80.5 all-reduce.8
  103.0 138.0 all-reduce.10
  313.0 152.1 all-reduce.14
  470.1 74.3 all-reduce.12
  620.4 86.9 all-reduce.16
